TPU v7x, 32 devices: a whole 2x2x4 slice. The times are simulated.
32 devices in a mesh: sub: 4 (over z), crow: 2 (over x), ccol: 4 (over y, core).
Axes of the slice: x: 2, y: 2, z: 4, core: 2. Of those that a mesh axis runs over, the one named last changes fastest.
Arguments:
- right_side: bfloat16 [32, 1536, 128], P(('sub', 'crow', 'ccol')), may hold values from -6 to 6
- stiff_diag: float32 [32, 1536], P(('sub', 'crow', 'ccol')), may hold values from 1 to 4
- dual_op: bfloat16 [32, 1536, 1536], P(('sub', 'crow', 'ccol')), may hold values from -0.15625 to 0.15625
- schur_op: bfloat16 [32, 1536, 1536], P(('sub', 'crow', 'ccol')), may hold values from -0.15625 to 0.15625
- modes: bfloat16 [32, 1536, 64], P(('sub', 'crow', 'ccol')), may hold values from -0.15625 to 0.15625
- coarse_inverse: bfloat16 [8, 4, 64, 8, 256], P(None, 'sub', None, ('crow', 'ccol')), may hold values from -0.125 to 0.125
- face_index: int32 [32, 2, 384], replicated, may hold values from 0 to 1535, as said below
Outputs:
- multipliers: float32 [32, 1536, 128], P(('sub', 'crow', 'ccol'))
- residual: bfloat16 [32, 1536, 128], P(('sub', 'crow', 'ccol'))
Inputs may be any that keep to these rules, and one draw needn't show every extreme that they name: `face_index`: for each subdomain its 768 entries are distinct.
All inputs are finite; a program needn't handle non-finite values.
Results may differ from a plain program's by a relative error of at most 0.0055.
Values may be sent and summed in bfloat16 or wider, within the bound.
A program may use at most 64 MiB of HBM per device.

v0:
```python
import functools

import jax
import jax.numpy as jnp
from jax import lax
from jax.experimental import pallas as pl
from jax.experimental.pallas import tpu as pltpu
from jax.sharding import PartitionSpec as P

spectrum_low = 0.5
spectrum_high = 4.0
center = (spectrum_high + spectrum_low) / 2.0
half_width = (spectrum_high - spectrum_low) / 2.0
ratio_old = half_width / center
ratio_new = 1.0 / (2.0 * center / half_width - ratio_old)
carry = ratio_new * ratio_old
gain = 2.0 * ratio_new / half_width

F32 = jnp.float32
BF16 = jnp.bfloat16
MESH = pl.DeviceIdType.MESH


def mm(left, right):
    return jnp.dot(left, right, preferred_element_type=F32)


def kernel(
    dims,
    rhs_h, diag_h, dual_h, schur_h, modes_h, coarse_h, face_h,
    mult, res,
    rhs, diag, dual, schur, modes_t, modes, coarse, face,
    rows_of, pick, put, vec, prod, base, step0, work, kz, hz,
    ag, part, rs, solved, near, ysend, yrecv, zsend, zrecv,
    in_sem, sch_sem, dua_sem, ag_s, ag_r, rs_s, rs_r, nb_s, nb_r, hy_s, hy_r, hz_s, hz_r,
):
    subs, crows, ccols = dims
    groups = crows * ccols
    m = rhs.shape[0]
    loads = ysend.shape[3]
    nm = modes.shape[1]
    face_n = face.shape[1]
    ch = 512 if m % 512 == 0 else m
    chunks = m // ch
    half = face_n // 2
    sub = lax.axis_index("sub")
    crow = lax.axis_index("crow")
    ccol = lax.axis_index("ccol")
    group = crow * ccols + ccol
    flat = sub * groups + group

    def local(src, dst, sem):
        return pltpu.make_async_copy(src, dst, sem)

    loads_in = [
        local(rhs_h.at[0], rhs.at[:, pl.ds(0, loads)], in_sem.at[0]),
        local(modes_h.at[0], modes_t, in_sem.at[1]),
        local(face_h.at[flat], face, in_sem.at[2]),
        local(diag_h, diag, in_sem.at[3]),
        local(coarse_h, coarse, in_sem.at[4]),
    ]
    sch_in = [
        local(schur_h.at[0, pl.ds(k * ch, ch)], schur.at[pl.ds(k * ch, ch)], sch_sem.at[k])
        for k in range(chunks)
    ]
    dua_in = [
        local(dual_h.at[0, pl.ds(k * ch, ch)], dual.at[pl.ds(k * ch, ch)], dua_sem.at[k])
        for k in range(chunks)
    ]
    for c in loads_in[:2] + sch_in + loads_in[2:]:
        c.start()

    def sub_id(s):
        return (s, crow, ccol)

    def group_id(g):
        return (sub, g // ccols, lax.rem(g, ccols))

    barrier = pltpu.get_barrier_semaphore()
    for d in range(1, subs):
        pl.semaphore_signal(
            barrier, inc=1, device_id=sub_id(lax.rem(sub + d, subs)), device_id_type=MESH
        )
    for d in range(1, groups):
        pl.semaphore_signal(
            barrier, inc=1, device_id=group_id(lax.rem(group + d, groups)), device_id_type=MESH
        )

    def remote(src, dst, s_sem, r_sem, dev):
        return pltpu.make_async_remote_copy(
            src_ref=src, dst_ref=dst, send_sem=s_sem, recv_sem=r_sem,
            device_id=dev, device_id_type=MESH,
        )

    gathers = [
        [
            remote(ag.at[t, sub], ag.at[t, sub], ag_s.at[t, d - 1], ag_r.at[t, d - 1],
                   sub_id(lax.rem(sub + d, subs)))
            for d in range(1, subs)
        ]
        for t in range(2)
    ]
    far = [ccols // 2] + [c for c in range(1, ccols) if c != ccols // 2]
    hops = [(r, c) for r in range(1, crows) for c in far + [0]] + [(0, c) for c in far]
    scatters = []
    for t in range(2):
        row = []
        for d, (dr, dc) in enumerate(hops):
            r, c = lax.rem(crow + dr, crows), lax.rem(ccol + dc, ccols)
            row.append(
                remote(part.at[t, r * ccols + c], rs.at[t, d], rs_s.at[t, d], rs_r.at[t, d],
                       (sub, r, c))
            )
        scatters.append(row)
    has_next = sub < subs - 1
    has_prev = sub > 0
    after = sub_id(jnp.minimum(sub + 1, subs - 1))
    before = sub_id(jnp.maximum(sub - 1, 0))
    ends = ((0, 1, after, has_next, has_prev), (1, 0, before, has_prev, has_next))

    def near_copy(t, e):
        return remote(solved.at[t], near.at[t, e], nb_s.at[t, e], nb_r.at[t, e], ends[e][2])

    def y_copy(t, e):
        return remote(ysend.at[t, ends[e][1]], yrecv.at[t, e], hy_s.at[t, e], hy_r.at[t, e],
                      ends[e][2])

    def z_copy(e):
        return remote(zsend.at[ends[e][1]], zrecv.at[e], hz_s.at[e], hz_r.at[e], ends[e][2])

    def send(make):
        for e in range(2):
            pl.when(ends[e][3])(lambda e=e: make(e).start())

    def arrive(make):
        for e in range(2):
            pl.when(ends[e][4])(lambda e=e: make(e).wait_recv())

    def drain(make):
        for e in range(2):
            pl.when(ends[e][3])(lambda e=e: make(e).wait_send())

    for e in range(2):

        @pl.when(jnp.logical_not(ends[e][4]))
        def _(e=e):
            zrecv[e] = jnp.zeros_like(zrecv[e])
            for t in range(2):
                yrecv[t, e] = jnp.zeros_like(yrecv[t, e])
                near[t, e] = jnp.zeros_like(near[t, e])

    def rows(k):
        return pl.ds(k * ch, ch)

    loads_in[0].wait()
    loads_in[1].wait()
    ag[0, sub] = mm(modes_t[...], rhs[:, :loads]).astype(BF16)
    loads_in[2].wait()
    lane = lax.broadcasted_iota(jnp.int32, (face_n, 128), 1)
    for e in range(2):
        wide = jnp.broadcast_to(face[e:e + 1, :], (128, face_n)).T
        for c in range(m // 128):
            pick[e * face_n:(e + 1) * face_n, c * 128:(c + 1) * 128] = jnp.where(
                wide == lane + c * 128, 1.0, 0.0
            ).astype(BF16)

    pl.semaphore_wait(barrier, subs - 1 + groups - 1)
    for c in gathers[0]:
        c.start()

    modes[...] = modes_t[...].T
    vec[:, loads:loads + nm] = modes[...]
    for k in range(chunks):
        sch_in[k].wait()
        dua_in[k].start()
    loads_in[3].wait()
    sub_row = lax.broadcasted_iota(jnp.int32, (128, face_n), 0)
    for c in range(m // 128):
        span = slice(c * 128, (c + 1) * 128)
        for e in range(2):
            put[span, e * face_n:(e + 1) * face_n] = jnp.where(
                face[e:e + 1, :] == sub_row + c * 128, 1.0, 0.0
            ).astype(BF16)
        rows_of[span, :] = jnp.broadcast_to(diag[:, span], (128, 128)).T

    for k in range(chunks):
        u = mm(schur[rows(k), :], rhs[:, :loads]) * (1.0 / center)
        step0[rows(k), :] = u
        vec[rows(k), :loads] = u.astype(BF16)

    for c in dua_in:
        c.wait()
    for k in range(chunks):
        y = mm(dual[rows(k), :], vec[...])
        prod[rows(k), :] = y[:, :loads]
        work[rows(k), :] = y.astype(BF16)
        kz[rows(k), :] = y[:, loads:].astype(BF16)
    def coarse_step(t):
        for c in gathers[t]:
            c.wait_recv()
        share = mm(coarse[...], ag[t].reshape(subs * nm, loads))
        part[t] = share.astype(BF16).reshape(groups, nm, loads)
        for c in scatters[t]:
            c.start()

    def coarse_end(t):
        total = part[t, group].astype(F32)
        for d in range(1, groups):
            scatters[t][d - 1].wait_recv()
            total = total + rs[t, d - 1].astype(F32)
        solved[t] = total.astype(BF16)
        send(functools.partial(near_copy, t))

    loads_in[4].wait()
    coarse_step(0)

    for e in range(2):
        got = mm(pick[e * face_n:(e + 1) * face_n, :], work[...])
        ysend[0, e] = got[:, :loads].astype(BF16)
        zsend[e] = jnp.concatenate(
            [got[:half, loads:], got[half:, loads:]], axis=1
        ).astype(BF16)
    send(functools.partial(y_copy, 0))
    send(z_copy)

    coarse_end(0)
    for k in range(chunks):
        p0 = step0[rows(k), :] + mm(modes[rows(k), :], solved[0]) * (1.0 / center)
        step0[rows(k), :] = p0
        base[rows(k), :] = (
            rhs[rows(k), :loads].astype(F32)
            - rows_of[rows(k), :] * p0
            - prod[rows(k), :]
            - mm(kz[rows(k), :nm], solved[0]) * (1.0 / center)
        )
    arrive(functools.partial(y_copy, 0))
    for k in range(chunks):
        base[rows(k), :] += mm(put[rows(k), :face_n], yrecv[0, 0]) + mm(
            put[rows(k), face_n:], yrecv[0, 1]
        )
    arrive(z_copy)
    for k in range(chunks):
        for e in range(2):
            low = e * face_n
            hz[e, rows(k), :] = (
                mm(put[rows(k), low:low + half], zrecv[e, :, :nm])
                + mm(put[rows(k), low + half:low + face_n], zrecv[e, :, nm:])
            ).astype(BF16)
    arrive(functools.partial(near_copy, 0))
    for k in range(chunks):
        r1 = base[rows(k), :] + (
            mm(hz[0, rows(k), :nm], near[0, 0]) + mm(hz[1, rows(k), :nm], near[0, 1])
        ) * (1.0 / center)
        base[rows(k), :] = r1
        vec[rows(k), :loads] = r1.astype(BF16)

    ag[1, sub] = mm(modes_t[...], vec[:, :loads]).astype(BF16)
    for c in gathers[1]:
        c.start()
    for k in range(chunks):
        w = carry * step0[rows(k), :] + gain * mm(schur[rows(k), :], vec[:, :loads])
        prod[rows(k), :] = w
        work[rows(k), :loads] = w.astype(BF16)
    for k in range(chunks):
        y = mm(dual[rows(k), :], work[:, :loads])
        base[rows(k), :] -= y
        vec[rows(k), :loads] = y.astype(BF16)
    coarse_step(1)
    for e in range(2):
        ysend[1, e] = mm(pick[e * face_n:(e + 1) * face_n, :], vec[:, :loads]).astype(BF16)
    send(functools.partial(y_copy, 1))
    coarse_end(1)
    for k in range(chunks):
        p1 = prod[rows(k), :] + gain * mm(modes[rows(k), :], solved[1])
        mult[rows(k), :] = step0[rows(k), :] + p1
        base[rows(k), :] -= rows_of[rows(k), :] * p1 + gain * mm(kz[rows(k), :nm], solved[1])
    arrive(functools.partial(y_copy, 1))
    for k in range(chunks):
        base[rows(k), :] += mm(put[rows(k), :face_n], yrecv[1, 0]) + mm(
            put[rows(k), face_n:], yrecv[1, 1]
        )
    arrive(functools.partial(near_copy, 1))
    for k in range(chunks):
        res[rows(k), :] = (
            base[rows(k), :]
            + gain * (mm(hz[0, rows(k), :nm], near[1, 0]) + mm(hz[1, rows(k), :nm], near[1, 1]))
        ).astype(BF16)
    for t in range(2):
        for c in gathers[t] + scatters[t]:
            c.wait_send()
        drain(functools.partial(y_copy, t))
        drain(functools.partial(near_copy, t))
    drain(z_copy)


def write_out(mult, res, mult_h, res_h, sem):
    copies = [
        pltpu.make_async_copy(mult, mult_h.at[0], sem.at[0]),
        pltpu.make_async_copy(res, res_h.at[0], sem.at[1]),
    ]
    for c in copies:
        c.start()
    for c in copies:
        c.wait()


def local(dims, right_side, stiff_diag, dual_op, schur_op, modes, coarse_inverse, face_index):
    subs, crows, ccols = dims
    groups = crows * ccols
    _, m, loads = right_side.shape
    nm = modes.shape[2]
    face_n = face_index.shape[2]
    coarse = coarse_inverse.reshape(
        coarse_inverse.shape[0] * coarse_inverse.shape[2], coarse_inverse.shape[4]
    )
    ch = 512 if m % 512 == 0 else m
    v = pltpu.VMEM
    dma = pltpu.SemaphoreType.DMA
    any_spec = pl.BlockSpec(memory_space=pl.ANY)
    mult, res = pl.pallas_call(
        functools.partial(kernel, dims),
        out_shape=(v((m, loads), F32), v((m, loads), BF16)),
        in_specs=[pl.BlockSpec(memory_space=pltpu.HBM)] * 7,
        out_specs=(pl.BlockSpec(memory_space=pltpu.VMEM),) * 2,
        scratch_shapes=[
            v((m, 2 * loads), BF16), v((1, m), F32), v((m, m), BF16), v((m, m), BF16),
            v((nm, m), BF16), v((m, nm), BF16), v(coarse.shape, BF16), v((2, face_n), jnp.int32),
            v((m, loads), F32), v((2 * face_n, m), BF16), v((m, 2 * face_n), BF16),
            v((m, loads + nm), BF16), v((m, loads), F32), v((m, loads), F32),
            v((m, loads), F32), v((m, loads + nm), BF16), v((m, nm), BF16), v((2, m, nm), BF16),
            v((2, subs, nm, loads), BF16), v((2, groups, nm, loads), BF16),
            v((2, groups - 1, nm, loads), BF16), v((2, nm, loads), BF16),
            v((2, 2, nm, loads), BF16), v((2, 2, face_n, loads), BF16),
            v((2, 2, face_n, loads), BF16), v((2, face_n // 2, 2 * nm), BF16), v((2, face_n // 2, 2 * nm), BF16),
            dma((5,)), dma((m // ch,)), dma((m // ch,)),
            dma((2, subs - 1)), dma((2, subs - 1)), dma((2, groups - 1)), dma((2, groups - 1)),
            dma((2, 2)), dma((2, 2)), dma((2, 2)), dma((2, 2)), dma((2,)), dma((2,)),
        ],
        compiler_params=pltpu.CompilerParams(
            collective_id=0, has_side_effects=True, vmem_limit_bytes=60 * 1024 * 1024
        ),
    )(right_side, stiff_diag, dual_op, schur_op, jnp.swapaxes(modes, 1, 2), coarse, face_index)
    return pl.pallas_call(
        write_out,
        out_shape=(
            jax.ShapeDtypeStruct((1, m, loads), F32),
            jax.ShapeDtypeStruct((1, m, loads), BF16),
        ),
        in_specs=[pl.BlockSpec(memory_space=pltpu.VMEM)] * 2,
        out_specs=(any_spec, any_spec),
        scratch_shapes=[dma((2,))],
        compiler_params=pltpu.CompilerParams(vmem_limit_bytes=1024 * 1024),
    )(mult, res)


def solution(mesh):
    dims = (mesh.shape["sub"], mesh.shape["crow"], mesh.shape["ccol"])
    in_specs = (
        P(("sub", "crow", "ccol"), None, None),
        P(("sub", "crow", "ccol"), None),
        P(("sub", "crow", "ccol"), None, None),
        P(("sub", "crow", "ccol"), None, None),
        P(("sub", "crow", "ccol"), None, None),
        P(None, "sub", None, ("crow", "ccol"), None),
        P(),
    )
    out_specs = (P(("sub", "crow", "ccol"), None, None), P(("sub", "crow", "ccol"), None, None))
    return jax.shard_map(
        functools.partial(local, dims), mesh=mesh, in_specs=in_specs, out_specs=out_specs,
        check_vma=False,
    )
```

profile of v0, /device:TPU:0, one launch (start us, length us, event | category | flops | bytes accessed | tf_op | source)
XLA Modules:
  0.0 31.1 jit_solution(6326487115071437759)
XLA Ops:
  0.6 29.4 %shard_map.86 = (f32[1536,128]{1,0:T(8,128)S(1)}, bf16[1536,128]{1,0:T(8,128)(2,1)S(1)}) custom-call(bf16[1,1536,128]{2,1,0:T(8,128)(2,1)} %rhs_h.1, f32[1,1536]{1,0:T(1,128)} %diag_h.1, bf16[1,1536,1536]{2,1,0:T(8,128)(2,1)} %dual_h.1, bf16[1,1536,1536]{2,1,0:T(8,128)(2,1)} %schur_h.1, bf16[1,64,1536]{2,1,0:T(8,128)(2,1)} %bitcast.3, ...), custom_call_target="tpu_custom_call" | custom-call | tf_op jit(solution)/shard_map/pallas_call | solution.py:320
  30.1 1.0 %shard_map.87 = (f32[1,1536,128]{2,1,0:T(8,128)}, bf16[1,1536,128]{2,1,0:T(8,128)(2,1)}) custom-call(f32[1536,128]{1,0:T(8,128)S(1)} %get-tuple-element.4.mult, bf16[1536,128]{1,0:T(8,128)(2,1)S(1)} %get-tuple-element.5.res), custom_call_target="tpu_custom_call" | custom-call | tf_op jit(solution)/shard_map/pallas_call | solution.py:343
where the time goes:
time: 31.2 us; the launch traced here: 31.1 us
  Pallas kernels  30.4 us (97%)
  between operations  0.64 us (2%)
    pallas_call x1, Pallas kernels, local(): pl.pallas_call(functools.partial(kernel, dims), out_shape=(v((m, loads),...  29.4 us
    pallas_call x1, Pallas kernels, local(): pl.pallas_call(write_out, out_shape=(jax.ShapeDtypeStruct((1, m, loads),...  1.02 us

commit v1 on v0

v1 whole, which is shorter than its diff:
```python
import functools

import jax
import jax.numpy as jnp
from jax import lax
from jax.experimental import pallas as pl
from jax.experimental.pallas import tpu as pltpu
from jax.sharding import PartitionSpec as P

spectrum_low = 0.5
spectrum_high = 4.0
center = (spectrum_high + spectrum_low) / 2.0
half_width = (spectrum_high - spectrum_low) / 2.0
ratio_old = half_width / center
ratio_new = 1.0 / (2.0 * center / half_width - ratio_old)
carry = ratio_new * ratio_old
gain = 2.0 * ratio_new / half_width

F32 = jnp.float32
BF16 = jnp.bfloat16
MESH = pl.DeviceIdType.MESH


def mm(left, right):
    return jnp.dot(left, right, preferred_element_type=F32)


def kernel(
    dims,
    rhs_h, diag_h, dual_h, schur_h, modes_h, coarse_h, face_h,
    mult, res,
    rhs, diag, dual, schur, modes_t, modes, coarse, face,
    rows_of, pick, put, vec, work, base, step0, prod, own, gh, kf, yz, bfull, cvec,
    ag0, agc, aga, bc, part, rs, solved, near, mft, mrecv, ysend, yrecv, zsend, zrecv,
    in_sem, sch_sem, dua_sem, ag_s, ag_r, rs_s, rs_r, nb_s, nb_r, hm_s, hm_r,
    hy_s, hy_r, hz_s, hz_r,
):
    subs, crows, ccols = dims
    groups = crows * ccols
    m = rhs.shape[0]
    loads = rhs.shape[1]
    nm = modes.shape[1]
    face_n = face.shape[1]
    ch = 512 if m % 512 == 0 else m
    chunks = m // ch
    half = face_n // 2
    inv = 1.0 / center
    sub = lax.axis_index("sub")
    crow = lax.axis_index("crow")
    ccol = lax.axis_index("ccol")
    group = crow * ccols + ccol
    flat = sub * groups + group

    def local(src, dst, sem):
        return pltpu.make_async_copy(src, dst, sem)

    loads_in = [
        local(rhs_h.at[0], rhs, in_sem.at[0]),
        local(modes_h.at[0], modes_t, in_sem.at[1]),
        local(face_h.at[flat], face, in_sem.at[2]),
        local(diag_h, diag, in_sem.at[3]),
        local(coarse_h, coarse, in_sem.at[4]),
    ]
    sch_in = [
        local(schur_h.at[0, pl.ds(k * ch, ch)], schur.at[pl.ds(k * ch, ch)], sch_sem.at[k])
        for k in range(chunks)
    ]
    dua_in = [
        local(dual_h.at[0, pl.ds(k * ch, ch)], dual.at[pl.ds(k * ch, ch)], dua_sem.at[k])
        for k in range(chunks)
    ]
    for c in loads_in[:3] + sch_in + loads_in[3:]:
        c.start()

    def sub_id(s):
        return (s, crow, ccol)

    def group_id(g):
        return (sub, g // ccols, lax.rem(g, ccols))

    barrier = pltpu.get_barrier_semaphore()
    for d in range(1, subs):
        pl.semaphore_signal(
            barrier, inc=1, device_id=sub_id(lax.rem(sub + d, subs)), device_id_type=MESH
        )
    for d in range(1, groups):
        pl.semaphore_signal(
            barrier, inc=1, device_id=group_id(lax.rem(group + d, groups)), device_id_type=MESH
        )

    def remote(src, dst, s_sem, r_sem, dev):
        return pltpu.make_async_remote_copy(
            src_ref=src, dst_ref=dst, send_sem=s_sem, recv_sem=r_sem,
            device_id=dev, device_id_type=MESH,
        )

    def gather(i, buf):
        return [
            remote(buf.at[sub], buf.at[sub], ag_s.at[i, d - 1], ag_r.at[i, d - 1],
                   sub_id(lax.rem(sub + d, subs)))
            for d in range(1, subs)
        ]

    gather0, gather_c, gather_a, gather_b = (
        gather(i, buf) for i, buf in enumerate((ag0, agc, aga, bc))
    )
    far = [ccols // 2] + [c for c in range(1, ccols) if c != ccols // 2]
    hops = [(r, c) for r in range(1, crows) for c in far + [0]] + [(0, c) for c in far]
    scatters = []
    for t in range(2):
        row = []
        for d, (dr, dc) in enumerate(hops):
            r, c = lax.rem(crow + dr, crows), lax.rem(ccol + dc, ccols)
            row.append(
                remote(part.at[t, r * ccols + c], rs.at[t, d], rs_s.at[t, d], rs_r.at[t, d],
                       (sub, r, c))
            )
        scatters.append(row)
    has_next = sub < subs - 1
    has_prev = sub > 0
    after = sub_id(jnp.minimum(sub + 1, subs - 1))
    before = sub_id(jnp.maximum(sub - 1, 0))
    ends = ((0, 1, after, has_next, has_prev), (1, 0, before, has_prev, has_next))

    def near_copy(e):
        return remote(solved, near.at[e], nb_s.at[e], nb_r.at[e], ends[e][2])

    def m_copy(e):
        return remote(mft.at[ends[e][1]], mrecv.at[e], hm_s.at[e], hm_r.at[e], ends[e][2])

    def y_copy(t, e):
        return remote(ysend.at[t, ends[e][1]], yrecv.at[t, e], hy_s.at[t, e], hy_r.at[t, e],
                      ends[e][2])

    def z_copy(e):
        return remote(zsend.at[ends[e][1]], zrecv.at[e], hz_s.at[e], hz_r.at[e], ends[e][2])

    def send(make):
        for e in range(2):
            pl.when(ends[e][3])(lambda e=e: make(e).start())

    def arrive(make):
        for e in range(2):
            pl.when(ends[e][4])(lambda e=e: make(e).wait_recv())

    def drain(make):
        for e in range(2):
            pl.when(ends[e][3])(lambda e=e: make(e).wait_send())

    for e in range(2):

        @pl.when(jnp.logical_not(ends[e][4]))
        def _(e=e):
            zrecv[e] = jnp.zeros_like(zrecv[e])
            mrecv[e] = jnp.zeros_like(mrecv[e])
            near[e] = jnp.zeros_like(near[e])
            for t in range(2):
                yrecv[t, e] = jnp.zeros_like(yrecv[t, e])

    def rows(k):
        return pl.ds(k * ch, ch)

    loads_in[0].wait()
    loads_in[1].wait()
    ag0[sub] = mm(modes_t[...], rhs[...]).astype(BF16)
    pl.semaphore_wait(barrier, subs - 1 + groups - 1)
    for c in gather0:
        c.start()

    loads_in[2].wait()
    lane = lax.broadcasted_iota(jnp.int32, (face_n, 128), 1)
    for e in range(2):
        wide = jnp.broadcast_to(face[e:e + 1, :], (128, face_n)).T
        for c in range(m // 128):
            pick[e * face_n:(e + 1) * face_n, c * 128:(c + 1) * 128] = jnp.where(
                wide == lane + c * 128, 1.0, 0.0
            ).astype(BF16)
    modes[...] = modes_t[...].T
    vec[:, loads:loads + nm] = modes[...]
    for e in range(2):
        mft[e] = mm(pick[e * face_n:(e + 1) * face_n, :], modes[...]).astype(BF16).T
    send(m_copy)

    for k in range(chunks):
        sch_in[k].wait()
        dua_in[k].start()
    for k in range(chunks):
        u = mm(schur[rows(k), :], rhs[...]) * inv
        step0[rows(k), :] = u
        vec[rows(k), :loads] = u.astype(BF16)

    loads_in[3].wait()
    sub_row = lax.broadcasted_iota(jnp.int32, (128, face_n), 0)
    for c in range(m // 128):
        span = slice(c * 128, (c + 1) * 128)
        for e in range(2):
            put[span, e * face_n:(e + 1) * face_n] = jnp.where(
                face[e:e + 1, :] == sub_row + c * 128, 1.0, 0.0
            ).astype(BF16)
        rows_of[span, :] = jnp.broadcast_to(diag[:, span], (128, 128)).T
    bfull[...] = jnp.zeros_like(bfull)

    for c in dua_in:
        c.wait()
    for k in range(chunks):
        y = mm(dual[rows(k), :], vec[...])
        work[rows(k), :] = y.astype(BF16)
        b = rhs[rows(k), :].astype(F32) - rows_of[rows(k), :] * step0[rows(k), :] - y[:, :loads]
        base[rows(k), :] = b
        own[rows(k), :] = b.astype(BF16)
        gh[rows(k), 2 * nm:] = (
            rows_of[rows(k), :nm] * modes[rows(k), :].astype(F32) + y[:, loads:]
        ).astype(BF16)
    for e in range(2):
        got = mm(pick[e * face_n:(e + 1) * face_n, :], work[...])
        ysend[0, e] = got[:, :loads].astype(BF16)
        faces = got[:, loads:].astype(BF16)
        kf[e] = faces
        zsend[e] = jnp.concatenate([faces[:half], faces[half:]], axis=1)
    send(functools.partial(y_copy, 0))
    send(z_copy)

    def scatter(t, coeff):
        part[t] = mm(coarse[...], coeff).astype(BF16).reshape(groups, nm, loads)
        for c in scatters[t]:
            c.start()

    def total(t):
        out = part[t, group].astype(F32)
        for d in range(1, groups):
            scatters[t][d - 1].wait_recv()
            out = out + rs[t, d - 1].astype(F32)
        return out.astype(BF16)

    loads_in[4].wait()
    for c in gather0:
        c.wait_recv()
    scatter(0, ag0[...].reshape(subs * nm, loads))

    plain = mm(modes_t[...], own[...])
    arrive(m_copy)
    bc[sub] = jnp.concatenate(
        [
            mm(mrecv[0], kf[0]) * inv,
            mm(modes_t[...], gh[:, 2 * nm:]) * (-inv),
            mm(mrecv[1], kf[1]) * inv,
        ],
        axis=1,
    ).astype(BF16)
    for c in gather_b:
        c.start()

    agc[sub] = total(0)
    for c in gather_c:
        c.start()
    arrive(functools.partial(y_copy, 0))
    aga[sub] = (plain + mm(mft[0], yrecv[0, 0]) + mm(mft[1], yrecv[0, 1])).astype(BF16)
    for c in gather_a:
        c.start()

    arrive(z_copy)
    blank = jnp.zeros((face_n, nm), BF16)
    for e in range(2):
        span = slice(e * face_n, (e + 1) * face_n)
        yz[span, :loads] = yrecv[0, e]
        z = jnp.concatenate([zrecv[e, :, :nm], zrecv[e, :, nm:]], axis=0)
        yz[span, loads:] = jnp.concatenate([z, blank] if e == 0 else [blank, z], axis=1)
    for k in range(chunks):
        got = mm(put[rows(k), :], yz[...])
        base[rows(k), :] += got[:, :loads]
        gh[rows(k), :2 * nm] = got[:, loads:].astype(BF16)
    for k in range(chunks):
        step0[rows(k), :] += mm(modes[rows(k), :], agc[sub]) * inv

    first, last = gather_c[0], gather_c[-1]
    if subs > 2:
        pl.when(has_prev)(first.wait_recv)
        pl.when(has_next)(last.wait_recv)
    elif subs == 2:
        first.wait_recv()
    cvec[:nm] = agc[jnp.maximum(sub - 1, 0)]
    cvec[nm:2 * nm] = agc[jnp.minimum(sub + 1, subs - 1)]
    cvec[2 * nm:] = -agc[sub]
    for k in range(chunks):
        r1 = base[rows(k), :] + mm(gh[rows(k), :], cvec[...]) * inv
        base[rows(k), :] = r1
        own[rows(k), :] = r1.astype(BF16)
    for k in range(chunks):
        w = carry * step0[rows(k), :] + gain * mm(schur[rows(k), :], own[...])
        prod[rows(k), :] = w
        vec[rows(k), :loads] = w.astype(BF16)

    for c in gather_b:
        c.wait_recv()
    for t in range(subs):
        for j, s in enumerate((t - 1, t, t + 1)):
            if 0 <= s < subs:
                bfull[s * nm:(s + 1) * nm, t * nm:(t + 1) * nm] = bc[t, :, j * nm:(j + 1) * nm]
    if subs > 2:
        pl.when(jnp.logical_not(has_prev))(first.wait_recv)
        pl.when(jnp.logical_not(has_next))(last.wait_recv)
        for c in gather_c[1:-1]:
            c.wait_recv()
    for c in gather_a:
        c.wait_recv()
    coeff = aga[...].reshape(subs * nm, loads).astype(F32) + mm(
        bfull[...], agc[...].reshape(subs * nm, loads)
    )
    scatter(1, coeff.astype(BF16))

    for k in range(chunks):
        y = mm(dual[rows(k), :], vec[:, :loads])
        base[rows(k), :] = base[rows(k), :] - y - rows_of[rows(k), :] * prod[rows(k), :]
        own[rows(k), :] = y.astype(BF16)
    for e in range(2):
        ysend[1, e] = mm(pick[e * face_n:(e + 1) * face_n, :], own[...]).astype(BF16)
    send(functools.partial(y_copy, 1))

    solved[...] = total(1)
    send(near_copy)
    for k in range(chunks):
        mult[rows(k), :] = (
            step0[rows(k), :] + prod[rows(k), :] + gain * mm(modes[rows(k), :], solved[...])
        )
        base[rows(k), :] -= gain * mm(gh[rows(k), 2 * nm:], solved[...])
    arrive(functools.partial(y_copy, 1))
    for k in range(chunks):
        base[rows(k), :] += mm(put[rows(k), :], yrecv[1].reshape(2 * face_n, loads))
    arrive(near_copy)
    for k in range(chunks):
        res[rows(k), :] = (
            base[rows(k), :]
            + gain * mm(gh[rows(k), :2 * nm], near[...].reshape(2 * nm, loads))
        ).astype(BF16)
    for c in gather0 + gather_c + gather_a + gather_b + scatters[0] + scatters[1]:
        c.wait_send()
    for t in range(2):
        drain(functools.partial(y_copy, t))
    drain(near_copy)
    drain(m_copy)
    drain(z_copy)


def write_out(mult, res, mult_h, res_h, sem):
    copies = [
        pltpu.make_async_copy(mult, mult_h.at[0], sem.at[0]),
        pltpu.make_async_copy(res, res_h.at[0], sem.at[1]),
    ]
    for c in copies:
        c.start()
    for c in copies:
        c.wait()


def local(dims, right_side, stiff_diag, dual_op, schur_op, modes, coarse_inverse, face_index):
    subs, crows, ccols = dims
    groups = crows * ccols
    _, m, loads = right_side.shape
    nm = modes.shape[2]
    face_n = face_index.shape[2]
    coarse = coarse_inverse.reshape(
        coarse_inverse.shape[0] * coarse_inverse.shape[2], coarse_inverse.shape[4]
    )
    ch = 512 if m % 512 == 0 else m
    v = pltpu.VMEM
    dma = pltpu.SemaphoreType.DMA
    any_spec = pl.BlockSpec(memory_space=pl.ANY)
    mult, res = pl.pallas_call(
        functools.partial(kernel, dims),
        out_shape=(v((m, loads), F32), v((m, loads), BF16)),
        in_specs=[pl.BlockSpec(memory_space=pltpu.HBM)] * 7,
        out_specs=(pl.BlockSpec(memory_space=pltpu.VMEM),) * 2,
        scratch_shapes=[
            v((m, loads), BF16), v((1, m), F32), v((m, m), BF16), v((m, m), BF16),
            v((nm, m), BF16), v((m, nm), BF16), v(coarse.shape, BF16), v((2, face_n), jnp.int32),
            v((m, loads), F32), v((2 * face_n, m), BF16), v((m, 2 * face_n), BF16),
            v((m, loads + nm), BF16), v((m, loads + nm), BF16), v((m, loads), F32),
            v((m, loads), F32), v((m, loads), F32), v((m, loads), BF16), v((m, 3 * nm), BF16),
            v((2, face_n, nm), BF16), v((2 * face_n, loads + 2 * nm), BF16),
            v((subs * nm, subs * nm), BF16), v((3 * nm, loads), BF16),
            v((subs, nm, loads), BF16), v((subs, nm, loads), BF16), v((subs, nm, loads), BF16),
            v((subs, nm, 3 * nm), BF16), v((2, groups, nm, loads), BF16),
            v((2, groups - 1, nm, loads), BF16), v((nm, loads), BF16),
            v((2, nm, loads), BF16), v((2, nm, face_n), BF16), v((2, nm, face_n), BF16),
            v((2, 2, face_n, loads), BF16), v((2, 2, face_n, loads), BF16),
            v((2, face_n // 2, 2 * nm), BF16), v((2, face_n // 2, 2 * nm), BF16),
            dma((5,)), dma((m // ch,)), dma((m // ch,)),
            dma((4, subs - 1)), dma((4, subs - 1)), dma((2, groups - 1)), dma((2, groups - 1)),
            dma((2,)), dma((2,)), dma((2,)), dma((2,)), dma((2, 2)), dma((2, 2)),
            dma((2,)), dma((2,)),
        ],
        compiler_params=pltpu.CompilerParams(
            collective_id=0, has_side_effects=True, vmem_limit_bytes=60 * 1024 * 1024
        ),
    )(right_side, stiff_diag, dual_op, schur_op, jnp.swapaxes(modes, 1, 2), coarse, face_index)
    return pl.pallas_call(
        write_out,
        out_shape=(
            jax.ShapeDtypeStruct((1, m, loads), F32),
            jax.ShapeDtypeStruct((1, m, loads), BF16),
        ),
        in_specs=[pl.BlockSpec(memory_space=pltpu.VMEM)] * 2,
        out_specs=(any_spec, any_spec),
        scratch_shapes=[dma((2,))],
        compiler_params=pltpu.CompilerParams(vmem_limit_bytes=1024 * 1024),
    )(mult, res)


def solution(mesh):
    dims = (mesh.shape["sub"], mesh.shape["crow"], mesh.shape["ccol"])
    in_specs = (
        P(("sub", "crow", "ccol"), None, None),
        P(("sub", "crow", "ccol"), None),
        P(("sub", "crow", "ccol"), None, None),
        P(("sub", "crow", "ccol"), None, None),
        P(("sub", "crow", "ccol"), None, None),
        P(None, "sub", None, ("crow", "ccol"), None),
        P(),
    )
    out_specs = (P(("sub", "crow", "ccol"), None, None), P(("sub", "crow", "ccol"), None, None))
    return jax.shard_map(
        functools.partial(local, dims), mesh=mesh, in_specs=in_specs, out_specs=out_specs,
        check_vma=False,
    )
```

time: 31.2 us -> 34.6 us (1.11)
  Pallas kernels: 30.4 us -> 33.8 us
    pallas_call x1, Pallas kernels: 29.4 us -> 32.8 us  [local(): pl.pallas_call(functools.partial(kernel, dims), out_shape=(v((m, loads),...]
where the time goes in v1:
time: 34.6 us; the launch traced here: 34.5 us
  Pallas kernels  33.8 us (98%)
  between operations  0.64 us (2%)
    pallas_call x1, Pallas kernels, local(): pl.pallas_call(functools.partial(kernel, dims), out_shape=(v((m, loads),...  32.8 us
    pallas_call x1, Pallas kernels, local(): pl.pallas_call(write_out, out_shape=(jax.ShapeDtypeStruct((1, m, loads),...  1.02 us

profile of v1, /device:TPU:0, one launch (start us, length us, event | category | flops | bytes accessed | tf_op | source)
XLA Modules:
  0.0 34.5 jit_solution(17433962535395085815)
XLA Ops:
  0.6 32.8 %shard_map.86 = (f32[1536,128]{1,0:T(8,128)S(1)}, bf16[1536,128]{1,0:T(8,128)(2,1)S(1)}) custom-call(bf16[1,1536,128]{2,1,0:T(8,128)(2,1)} %rhs_h.1, f32[1,1536]{1,0:T(1,128)} %diag_h.1, bf16[1,1536,1536]{2,1,0:T(8,128)(2,1)} %dual_h.1, bf16[1,1536,1536]{2,1,0:T(8,128)(2,1)} %schur_h.1, bf16[1,64,1536]{2,1,0:T(8,128)(2,1)} %bitcast.3, ...), custom_call_target="tpu_custom_call" | custom-call | tf_op jit(solution)/shard_map/pallas_call | solution.py:368
  33.4 1.0 %shard_map.87 = (f32[1,1536,128]{2,1,0:T(8,128)}, bf16[1,1536,128]{2,1,0:T(8,128)(2,1)}) custom-call(f32[1536,128]{1,0:T(8,128)S(1)} %get-tuple-element.4.mult, bf16[1536,128]{1,0:T(8,128)(2,1)S(1)} %get-tuple-element.5.res), custom_call_target="tpu_custom_call" | custom-call | tf_op jit(solution)/shard_map/pallas_call | solution.py:396

commit v2 on v1

--- a/solution.py
+++ b/solution.py
@@ -30,9 +30,9 @@
     rhs_h, diag_h, dual_h, schur_h, modes_h, coarse_h, face_h,
     mult, res,
     rhs, diag, dual, schur, modes_t, modes, coarse, face,
-    rows_of, pick, put, vec, work, base, step0, prod, own, gh, kf, yz, bfull, cvec,
-    ag0, agc, aga, bc, part, rs, solved, near, mft, mrecv, ysend, yrecv, zsend, zrecv,
-    in_sem, sch_sem, dua_sem, ag_s, ag_r, rs_s, rs_r, nb_s, nb_r, hm_s, hm_r,
+    rows_of, pick, put, vec, work, base, step0, prod, own, gh, yz, cvec,
+    ag, part, rs, solved, near, mf, mft, ysend, yrecv, zsend, zrecv,
+    in_sem, sch_sem, dua_sem, ag_s, ag_r, rs_s, rs_r, nb_s, nb_r,
     hy_s, hy_r, hz_s, hz_r,
 ):
     subs, crows, ccols = dims
@@ -94,16 +94,14 @@
             device_id=dev, device_id_type=MESH,
         )
 
-    def gather(i, buf):
-        return [
-            remote(buf.at[sub], buf.at[sub], ag_s.at[i, d - 1], ag_r.at[i, d - 1],
+    gathers = [
+        [
+            remote(ag.at[t, sub], ag.at[t, sub], ag_s.at[t, d - 1], ag_r.at[t, d - 1],
                    sub_id(lax.rem(sub + d, subs)))
             for d in range(1, subs)
         ]
-
-    gather0, gather_c, gather_a, gather_b = (
-        gather(i, buf) for i, buf in enumerate((ag0, agc, aga, bc))
-    )
+        for t in range(2)
+    ]
     far = [ccols // 2] + [c for c in range(1, ccols) if c != ccols // 2]
     hops = [(r, c) for r in range(1, crows) for c in far + [0]] + [(0, c) for c in far]
     scatters = []
@@ -122,11 +120,8 @@
     before = sub_id(jnp.maximum(sub - 1, 0))
     ends = ((0, 1, after, has_next, has_prev), (1, 0, before, has_prev, has_next))
 
-    def near_copy(e):
-        return remote(solved, near.at[e], nb_s.at[e], nb_r.at[e], ends[e][2])
-
-    def m_copy(e):
-        return remote(mft.at[ends[e][1]], mrecv.at[e], hm_s.at[e], hm_r.at[e], ends[e][2])
+    def near_copy(t, e):
+        return remote(solved.at[t], near.at[t, e], nb_s.at[t, e], nb_r.at[t, e], ends[e][2])
 
     def y_copy(t, e):
         return remote(ysend.at[t, ends[e][1]], yrecv.at[t, e], hy_s.at[t, e], hy_r.at[t, e],
@@ -152,9 +147,8 @@
         @pl.when(jnp.logical_not(ends[e][4]))
         def _(e=e):
             zrecv[e] = jnp.zeros_like(zrecv[e])
-            mrecv[e] = jnp.zeros_like(mrecv[e])
-            near[e] = jnp.zeros_like(near[e])
             for t in range(2):
+                near[t, e] = jnp.zeros_like(near[t, e])
                 yrecv[t, e] = jnp.zeros_like(yrecv[t, e])
 
     def rows(k):
@@ -162,9 +156,9 @@
 
     loads_in[0].wait()
     loads_in[1].wait()
-    ag0[sub] = mm(modes_t[...], rhs[...]).astype(BF16)
+    ag[0, sub] = mm(modes_t[...], rhs[...]).astype(BF16)
     pl.semaphore_wait(barrier, subs - 1 + groups - 1)
-    for c in gather0:
+    for c in gathers[0]:
         c.start()
 
     loads_in[2].wait()
@@ -177,9 +171,7 @@
             ).astype(BF16)
     modes[...] = modes_t[...].T
     vec[:, loads:loads + nm] = modes[...]
-    for e in range(2):
-        mft[e] = mm(pick[e * face_n:(e + 1) * face_n, :], modes[...]).astype(BF16).T
-    send(m_copy)
+    work[:, loads + nm:] = modes[...]
 
     for k in range(chunks):
         sch_in[k].wait()
@@ -188,6 +180,37 @@
         u = mm(schur[rows(k), :], rhs[...]) * inv
         step0[rows(k), :] = u
         vec[rows(k), :loads] = u.astype(BF16)
+
+    def scatter(t):
+        for c in gathers[t]:
+            c.wait_recv()
+        part[t] = mm(coarse[...], ag[t].reshape(subs * nm, loads)).astype(BF16).reshape(groups, nm, loads)
+        for c in scatters[t]:
+            c.start()
+
+    def total(t):
+        out = part[t, group].astype(F32)
+        for d in range(1, groups):
+            scatters[t][d - 1].wait_recv()
+            out = out + rs[t, d - 1].astype(F32)
+        return out.astype(BF16)
+
+    for c in dua_in:
+        c.wait()
+    for k in range(chunks):
+        y = mm(dual[rows(k), :], vec[...])
+        prod[rows(k), :] = y[:, :loads]
+        work[rows(k), :loads + nm] = y.astype(BF16)
+    for e in range(2):
+        got = mm(pick[e * face_n:(e + 1) * face_n, :], work[...])
+        ysend[0, e] = got[:, :loads].astype(BF16)
+        faces = got[:, loads:loads + nm].astype(BF16)
+        zsend[e] = jnp.concatenate([faces[:half], faces[half:]], axis=1)
+        mf[e] = got[:, loads + nm:].astype(BF16)
+    send(functools.partial(y_copy, 0))
+    send(z_copy)
+    loads_in[4].wait()
+    scatter(0)
 
     loads_in[3].wait()
     sub_row = lax.broadcasted_iota(jnp.int32, (128, face_n), 0)
@@ -198,66 +221,25 @@
                 face[e:e + 1, :] == sub_row + c * 128, 1.0, 0.0
             ).astype(BF16)
         rows_of[span, :] = jnp.broadcast_to(diag[:, span], (128, 128)).T
-    bfull[...] = jnp.zeros_like(bfull)
-
-    for c in dua_in:
-        c.wait()
-    for k in range(chunks):
-        y = mm(dual[rows(k), :], vec[...])
-        work[rows(k), :] = y.astype(BF16)
-        b = rhs[rows(k), :].astype(F32) - rows_of[rows(k), :] * step0[rows(k), :] - y[:, :loads]
+
+    for e in range(2):
+        mft[e] = mf[e].T
+    for k in range(chunks):
+        b = rhs[rows(k), :].astype(F32) - rows_of[rows(k), :] * step0[rows(k), :] - prod[rows(k), :]
         base[rows(k), :] = b
         own[rows(k), :] = b.astype(BF16)
         gh[rows(k), 2 * nm:] = (
-            rows_of[rows(k), :nm] * modes[rows(k), :].astype(F32) + y[:, loads:]
+            rows_of[rows(k), :nm] * modes[rows(k), :].astype(F32)
+            + work[rows(k), loads:loads + nm].astype(F32)
         ).astype(BF16)
-    for e in range(2):
-        got = mm(pick[e * face_n:(e + 1) * face_n, :], work[...])
-        ysend[0, e] = got[:, :loads].astype(BF16)
-        faces = got[:, loads:].astype(BF16)
-        kf[e] = faces
-        zsend[e] = jnp.concatenate([faces[:half], faces[half:]], axis=1)
-    send(functools.partial(y_copy, 0))
-    send(z_copy)
-
-    def scatter(t, coeff):
-        part[t] = mm(coarse[...], coeff).astype(BF16).reshape(groups, nm, loads)
-        for c in scatters[t]:
-            c.start()
-
-    def total(t):
-        out = part[t, group].astype(F32)
-        for d in range(1, groups):
-            scatters[t][d - 1].wait_recv()
-            out = out + rs[t, d - 1].astype(F32)
-        return out.astype(BF16)
-
-    loads_in[4].wait()
-    for c in gather0:
-        c.wait_recv()
-    scatter(0, ag0[...].reshape(subs * nm, loads))
-
     plain = mm(modes_t[...], own[...])
-    arrive(m_copy)
-    bc[sub] = jnp.concatenate(
-        [
-            mm(mrecv[0], kf[0]) * inv,
-            mm(modes_t[...], gh[:, 2 * nm:]) * (-inv),
-            mm(mrecv[1], kf[1]) * inv,
-        ],
-        axis=1,
-    ).astype(BF16)
-    for c in gather_b:
-        c.start()
-
-    agc[sub] = total(0)
-    for c in gather_c:
-        c.start()
+    tie = mm(modes_t[...], gh[:, 2 * nm:]) * -inv
+    solved[0] = total(0)
+    send(functools.partial(near_copy, 0))
+    for k in range(chunks):
+        step0[rows(k), :] += mm(modes[rows(k), :], solved[0]) * inv
     arrive(functools.partial(y_copy, 0))
-    aga[sub] = (plain + mm(mft[0], yrecv[0, 0]) + mm(mft[1], yrecv[0, 1])).astype(BF16)
-    for c in gather_a:
-        c.start()
-
+    plain = plain + mm(mft[0], yrecv[0, 0]) + mm(mft[1], yrecv[0, 1])
     arrive(z_copy)
     blank = jnp.zeros((face_n, nm), BF16)
     for e in range(2):
@@ -265,23 +247,23 @@
         yz[span, :loads] = yrecv[0, e]
         z = jnp.concatenate([zrecv[e, :, :nm], zrecv[e, :, nm:]], axis=0)
         yz[span, loads:] = jnp.concatenate([z, blank] if e == 0 else [blank, z], axis=1)
+    ties = jnp.concatenate(
+        [mm(mft[e], yz[e * face_n:(e + 1) * face_n, loads + e * nm:loads + (e + 1) * nm]) * inv
+         for e in range(2)] + [tie],
+        axis=1,
+    ).astype(BF16)
+    arrive(functools.partial(near_copy, 0))
+    cvec[:2 * nm] = near[0].reshape(2 * nm, loads)
+    cvec[2 * nm:] = solved[0]
+    ag[1, sub] = (plain + mm(ties, cvec[...])).astype(BF16)
+    for c in gathers[1]:
+        c.start()
+    cvec[2 * nm:] = -solved[0]
     for k in range(chunks):
         got = mm(put[rows(k), :], yz[...])
         base[rows(k), :] += got[:, :loads]
         gh[rows(k), :2 * nm] = got[:, loads:].astype(BF16)
     for k in range(chunks):
-        step0[rows(k), :] += mm(modes[rows(k), :], agc[sub]) * inv
-
-    first, last = gather_c[0], gather_c[-1]
-    if subs > 2:
-        pl.when(has_prev)(first.wait_recv)
-        pl.when(has_next)(last.wait_recv)
-    elif subs == 2:
-        first.wait_recv()
-    cvec[:nm] = agc[jnp.maximum(sub - 1, 0)]
-    cvec[nm:2 * nm] = agc[jnp.minimum(sub + 1, subs - 1)]
-    cvec[2 * nm:] = -agc[sub]
-    for k in range(chunks):
         r1 = base[rows(k), :] + mm(gh[rows(k), :], cvec[...]) * inv
         base[rows(k), :] = r1
         own[rows(k), :] = r1.astype(BF16)
@@ -290,24 +272,7 @@
         prod[rows(k), :] = w
         vec[rows(k), :loads] = w.astype(BF16)
 
-    for c in gather_b:
-        c.wait_recv()
-    for t in range(subs):
-        for j, s in enumerate((t - 1, t, t + 1)):
-            if 0 <= s < subs:
-                bfull[s * nm:(s + 1) * nm, t * nm:(t + 1) * nm] = bc[t, :, j * nm:(j + 1) * nm]
-    if subs > 2:
-        pl.when(jnp.logical_not(has_prev))(first.wait_recv)
-        pl.when(jnp.logical_not(has_next))(last.wait_recv)
-        for c in gather_c[1:-1]:
-            c.wait_recv()
-    for c in gather_a:
-        c.wait_recv()
-    coeff = aga[...].reshape(subs * nm, loads).astype(F32) + mm(
-        bfull[...], agc[...].reshape(subs * nm, loads)
-    )
-    scatter(1, coeff.astype(BF16))
-
+    scatter(1)
     for k in range(chunks):
         y = mm(dual[rows(k), :], vec[:, :loads])
         base[rows(k), :] = base[rows(k), :] - y - rows_of[rows(k), :] * prod[rows(k), :]
@@ -316,28 +281,27 @@
         ysend[1, e] = mm(pick[e * face_n:(e + 1) * face_n, :], own[...]).astype(BF16)
     send(functools.partial(y_copy, 1))
 
-    solved[...] = total(1)
-    send(near_copy)
+    solved[1] = total(1)
+    send(functools.partial(near_copy, 1))
     for k in range(chunks):
         mult[rows(k), :] = (
-            step0[rows(k), :] + prod[rows(k), :] + gain * mm(modes[rows(k), :], solved[...])
+            step0[rows(k), :] + prod[rows(k), :] + gain * mm(modes[rows(k), :], solved[1])
         )
-        base[rows(k), :] -= gain * mm(gh[rows(k), 2 * nm:], solved[...])
+        base[rows(k), :] -= gain * mm(gh[rows(k), 2 * nm:], solved[1])
     arrive(functools.partial(y_copy, 1))
     for k in range(chunks):
         base[rows(k), :] += mm(put[rows(k), :], yrecv[1].reshape(2 * face_n, loads))
-    arrive(near_copy)
+    arrive(functools.partial(near_copy, 1))
     for k in range(chunks):
         res[rows(k), :] = (
             base[rows(k), :]
-            + gain * mm(gh[rows(k), :2 * nm], near[...].reshape(2 * nm, loads))
+            + gain * mm(gh[rows(k), :2 * nm], near[1].reshape(2 * nm, loads))
         ).astype(BF16)
-    for c in gather0 + gather_c + gather_a + gather_b + scatters[0] + scatters[1]:
-        c.wait_send()
     for t in range(2):
+        for c in gathers[t] + scatters[t]:
+            c.wait_send()
         drain(functools.partial(y_copy, t))
-    drain(near_copy)
-    drain(m_copy)
+        drain(functools.partial(near_copy, t))
     drain(z_copy)
 
 
@@ -374,20 +338,17 @@
             v((m, loads), BF16), v((1, m), F32), v((m, m), BF16), v((m, m), BF16),
             v((nm, m), BF16), v((m, nm), BF16), v(coarse.shape, BF16), v((2, face_n), jnp.int32),
             v((m, loads), F32), v((2 * face_n, m), BF16), v((m, 2 * face_n), BF16),
-            v((m, loads + nm), BF16), v((m, loads + nm), BF16), v((m, loads), F32),
+            v((m, loads + nm), BF16), v((m, loads + 2 * nm), BF16), v((m, loads), F32),
             v((m, loads), F32), v((m, loads), F32), v((m, loads), BF16), v((m, 3 * nm), BF16),
-            v((2, face_n, nm), BF16), v((2 * face_n, loads + 2 * nm), BF16),
-            v((subs * nm, subs * nm), BF16), v((3 * nm, loads), BF16),
-            v((subs, nm, loads), BF16), v((subs, nm, loads), BF16), v((subs, nm, loads), BF16),
-            v((subs, nm, 3 * nm), BF16), v((2, groups, nm, loads), BF16),
-            v((2, groups - 1, nm, loads), BF16), v((nm, loads), BF16),
-            v((2, nm, loads), BF16), v((2, nm, face_n), BF16), v((2, nm, face_n), BF16),
+            v((2 * face_n, loads + 2 * nm), BF16), v((3 * nm, loads), BF16),
+            v((2, subs, nm, loads), BF16), v((2, groups, nm, loads), BF16),
+            v((2, groups - 1, nm, loads), BF16), v((2, nm, loads), BF16),
+            v((2, 2, nm, loads), BF16), v((2, face_n, nm), BF16), v((2, nm, face_n), BF16),
             v((2, 2, face_n, loads), BF16), v((2, 2, face_n, loads), BF16),
             v((2, face_n // 2, 2 * nm), BF16), v((2, face_n // 2, 2 * nm), BF16),
             dma((5,)), dma((m // ch,)), dma((m // ch,)),
-            dma((4, subs - 1)), dma((4, subs - 1)), dma((2, groups - 1)), dma((2, groups - 1)),
-            dma((2,)), dma((2,)), dma((2,)), dma((2,)), dma((2, 2)), dma((2, 2)),
-            dma((2,)), dma((2,)),
+            dma((2, subs - 1)), dma((2, subs - 1)), dma((2, groups - 1)), dma((2, groups - 1)),
+            dma((2, 2)), dma((2, 2)), dma((2, 2)), dma((2, 2)), dma((2,)), dma((2,)),
         ],
         compiler_params=pltpu.CompilerParams(
             collective_id=0, has_side_effects=True, vmem_limit_bytes=60 * 1024 * 1024

time: 34.6 us -> 31.4 us (0.908)
  Pallas kernels: 33.8 us -> 30.6 us
    pallas_call x1, Pallas kernels: 32.8 us -> 29.6 us  [local(): pl.pallas_call(functools.partial(kernel, dims), out_shape=(v((m, loads),...]
where the time goes in v2:
time: 31.4 us; the launch traced here: 31.2 us
  Pallas kernels  30.6 us (97%)
  between operations  0.64 us (2%)
    pallas_call x1, Pallas kernels, local(): pl.pallas_call(functools.partial(kernel, dims), out_shape=(v((m, loads),...  29.6 us
    pallas_call x1, Pallas kernels, local(): pl.pallas_call(write_out, out_shape=(jax.ShapeDtypeStruct((1, m, loads),...  1.02 us

profile of v2, /device:TPU:0, one launch (start us, length us, event | category | flops | bytes accessed | tf_op | source)
XLA Modules:
  0.0 31.2 jit_solution(4790441718389123282)
XLA Ops:
  0.6 29.6 %shard_map.86 = (f32[1536,128]{1,0:T(8,128)S(1)}, bf16[1536,128]{1,0:T(8,128)(2,1)S(1)}) custom-call(bf16[1,1536,128]{2,1,0:T(8,128)(2,1)} %rhs_h.1, f32[1,1536]{1,0:T(1,128)} %diag_h.1, bf16[1,1536,1536]{2,1,0:T(8,128)(2,1)} %dual_h.1, bf16[1,1536,1536]{2,1,0:T(8,128)(2,1)} %schur_h.1, bf16[1,64,1536]{2,1,0:T(8,128)(2,1)} %bitcast.3, ...), custom_call_target="tpu_custom_call" | custom-call | tf_op jit(solution)/shard_map/pallas_call | solution.py:332
  30.2 1.0 %shard_map.87 = (f32[1,1536,128]{2,1,0:T(8,128)}, bf16[1,1536,128]{2,1,0:T(8,128)(2,1)}) custom-call(f32[1536,128]{1,0:T(8,128)S(1)} %get-tuple-element.4.mult, bf16[1536,128]{1,0:T(8,128)(2,1)S(1)} %get-tuple-element.5.res), custom_call_target="tpu_custom_call" | custom-call | tf_op jit(solution)/shard_map/pallas_call | solution.py:357

commit v3 on v2

--- a/solution.py
+++ b/solution.py
@@ -195,6 +195,9 @@
             out = out + rs[t, d - 1].astype(F32)
         return out.astype(BF16)
 
+    loads_in[4].wait()
+    scatter(0)
+
     for c in dua_in:
         c.wait()
     for k in range(chunks):
@@ -209,9 +212,6 @@
         mf[e] = got[:, loads + nm:].astype(BF16)
     send(functools.partial(y_copy, 0))
     send(z_copy)
-    loads_in[4].wait()
-    scatter(0)
-
     loads_in[3].wait()
     sub_row = lax.broadcasted_iota(jnp.int32, (128, face_n), 0)
     for c in range(m // 128):
@@ -222,6 +222,8 @@
             ).astype(BF16)
         rows_of[span, :] = jnp.broadcast_to(diag[:, span], (128, 128)).T
 
+    solved[0] = total(0)
+    send(functools.partial(near_copy, 0))
     for e in range(2):
         mft[e] = mf[e].T
     for k in range(chunks):
@@ -234,8 +236,6 @@
         ).astype(BF16)
     plain = mm(modes_t[...], own[...])
     tie = mm(modes_t[...], gh[:, 2 * nm:]) * -inv
-    solved[0] = total(0)
-    send(functools.partial(near_copy, 0))
     for k in range(chunks):
         step0[rows(k), :] += mm(modes[rows(k), :], solved[0]) * inv
     arrive(functools.partial(y_copy, 0))

time: 31.4 us -> 30.9 us (0.984)
  Pallas kernels: 30.6 us -> 30.2 us
    pallas_call x1, Pallas kernels: 29.6 us -> 29.1 us  [local(): pl.pallas_call(functools.partial(kernel, dims), out_shape=(v((m, loads),...]
where the time goes in v3:
time: 30.9 us; the launch traced here: 30.8 us
  Pallas kernels  30.2 us (98%)
  between operations  0.64 us (2%)
    pallas_call x1, Pallas kernels, local(): pl.pallas_call(functools.partial(kernel, dims), out_shape=(v((m, loads),...  29.1 us
    pallas_call x1, Pallas kernels, local(): pl.pallas_call(write_out, out_shape=(jax.ShapeDtypeStruct((1, m, loads),...  1.02 us

profile of v3, /device:TPU:0, one launch (start us, length us, event | category | flops | bytes accessed | tf_op | source)
XLA Modules:
  0.0 30.8 jit_solution(13105217392450049465)
XLA Ops:
  0.6 29.1 %shard_map.86 = (f32[1536,128]{1,0:T(8,128)S(1)}, bf16[1536,128]{1,0:T(8,128)(2,1)S(1)}) custom-call(bf16[1,1536,128]{2,1,0:T(8,128)(2,1)} %rhs_h.1, f32[1,1536]{1,0:T(1,128)} %diag_h.1, bf16[1,1536,1536]{2,1,0:T(8,128)(2,1)} %dual_h.1, bf16[1,1536,1536]{2,1,0:T(8,128)(2,1)} %schur_h.1, bf16[1,64,1536]{2,1,0:T(8,128)(2,1)} %bitcast.3, ...), custom_call_target="tpu_custom_call" | custom-call | tf_op jit(solution)/shard_map/pallas_call | solution.py:332
  29.8 1.0 %shard_map.87 = (f32[1,1536,128]{2,1,0:T(8,128)}, bf16[1,1536,128]{2,1,0:T(8,128)(2,1)}) custom-call(f32[1536,128]{1,0:T(8,128)S(1)} %get-tuple-element.4.mult, bf16[1536,128]{1,0:T(8,128)(2,1)S(1)} %get-tuple-element.5.res), custom_call_target="tpu_custom_call" | custom-call | tf_op jit(solution)/shard_map/pallas_call | solution.py:357
